TPU v7x, 256 devices: a whole 4x4x8 slice. The times are simulated.
256 devices in a mesh: rows: 64 (over z_hi, y, x, core), ch: 4 (over z_lo).
Axes of the slice: x: 4, y: 4, z: 8 (z_hi: 2, z_lo: 4; z = z_hi * 4 + z_lo), core: 2. Of those that a mesh axis runs over, the one named last changes fastest.
Arguments:
- pixels: bfloat16 [256, 96, 2048], P('rows', 'ch'), may hold values from -6 to 6
- depth_weight: float32 [96, 9], P('ch'), may hold values from -2 to 2
- mix_weight: bfloat16 [96, 96], replicated, may hold values from -0.625 to 0.625
- spectral_real: bfloat16 [256, 96, 1024], P(None, 'ch', 'rows'), may hold values from -4 to 4
- spectral_imag: bfloat16 [256, 96, 1024], P(None, 'ch', 'rows'), may hold values from -4 to 4
- query_weight: bfloat16 [96, 128], P('ch'), may hold values from -0.625 to 0.625
- key_weight: bfloat16 [96, 128], P('ch'), may hold values from -0.625 to 0.625
- query_pixels: int32 [4096], P('rows'), may hold values from 0 to 8191
- key_pixels: int32 [16384], P('rows'), may hold values from 0 to 8191
- positives: int32 [4096], P('rows'), may hold values from 0 to 16383
Outputs:
- encoded: bfloat16 [256, 96, 2048], P('rows', 'ch')
- losses: float32 [4096], P(('rows', 'ch'))
Inputs may be any that keep to these rules, and one draw needn't show every extreme that they name: `query_pixels`: each entry is r * 2048 + x for a pixel at row r and column x of the query's own slab of 4 rows. `key_pixels`: each entry is r * 2048 + x for a pixel at row r and column x of the key's own slab of 4 rows. `positives`: the number of the positive key among all 16384 keys, numbered slab by slab in the order of key_pixels.
All inputs are finite; a program needn't handle non-finite values.
Results may differ from a plain program's by a relative error of at most 0.0065.
Values may be sent and summed in bfloat16 or wider, within the bound.
A program may use at most 64 MiB of HBM per device.

v0:
```python
import jax
import jax.numpy as jnp
from jax import lax
from jax.sharding import PartitionSpec as P

DILATION = 2
score_scale = 10.0
exact = lax.Precision.HIGHEST


def extended(cells, sides, width):
    for axis, dim in sides:
        count = lax.axis_size(axis)
        ends = count - 1
        head = lax.slice_in_dim(cells, 0, width, axis=dim)
        tail = lax.slice_in_dim(cells, cells.shape[dim] - width, cells.shape[dim], axis=dim)
        cells = jnp.concatenate(
            [
                lax.ppermute(tail, axis, [(i, (i + 1) % count) for i in range(ends)]),
                cells,
                lax.ppermute(head, axis, [((i + 1) % count, i) for i in range(ends)]),
            ],
            axis=dim,
        )
    return cells


def unit_rows(values):
    return values * lax.rsqrt(jnp.sum(values * values, axis=1, keepdims=True) + 1e-06)


def angle_table(left_len, right_len, length, direction):
    left_index = lax.broadcasted_iota(jnp.int32, (left_len, right_len), 0)
    right_index = lax.broadcasted_iota(jnp.int32, (left_len, right_len), 1)
    phase_turns = left_index * right_index % length
    angles = phase_turns.astype(jnp.float32) * (direction * 2.0 * jnp.pi / length)
    return (jnp.cos(angles), jnp.sin(angles))


def transform_last(real_part, imag_part, direction, real_only, lower_half):
    length = real_part.shape[-1]
    first_len = 1 << (length.bit_length() - 1) // 2
    second = length // first_len
    kept = second // 2 if lower_half else second
    leading = real_part.shape[:-1]
    cos_first, sin_first = angle_table(first_len, first_len, first_len, direction)
    cos_twist, sin_twist = angle_table(first_len, second, length, direction)
    cos_second, sin_second = angle_table(second, second, second, direction)
    cos_second = cos_second[:, :kept]
    sin_second = sin_second[:, :kept]

    def over_first(matrix, values):
        return jnp.einsum("ka,...ab->...kb", matrix, values, precision=exact)

    def over_second(values, matrix):
        return jnp.einsum("...kb,bm->...km", values, matrix, precision=exact)

    real_grid = real_part.reshape(leading + (first_len, second))
    if imag_part is None:
        segment_real = over_first(cos_first, real_grid)
        segment_imag = over_first(sin_first, real_grid)
    else:
        imag_grid = imag_part.reshape(leading + (first_len, second))
        segment_real = over_first(cos_first, real_grid) - over_first(sin_first, imag_grid)
        segment_imag = over_first(sin_first, real_grid) + over_first(cos_first, imag_grid)
    twisted_real = segment_real * cos_twist - segment_imag * sin_twist
    twisted_imag = segment_real * sin_twist + segment_imag * cos_twist
    result_real = over_second(twisted_real, cos_second) - over_second(twisted_imag, sin_second)
    result_real = jnp.swapaxes(result_real, -1, -2).reshape(leading + (kept * first_len,))
    if real_only:
        return result_real
    result_imag = over_second(twisted_real, sin_second) + over_second(twisted_imag, cos_second)
    result_imag = jnp.swapaxes(result_imag, -1, -2).reshape(leading + (kept * first_len,))
    return (result_real, result_imag)


def transform_first(real_part, imag_part, direction):
    moved_real = jnp.moveaxis(real_part, 0, -1)
    moved_imag = jnp.moveaxis(imag_part, 0, -1)
    result_real, result_imag = transform_last(moved_real, moved_imag, direction, False, False)
    return (jnp.moveaxis(result_real, -1, 0), jnp.moveaxis(result_imag, -1, 0))


def score_fold(query_unit, targets, key_number):

    def add_block(carried, shard_piece, offset):
        scores = (
            jnp.einsum("qd,kd->qk", query_unit, shard_piece, preferred_element_type=jnp.float32)
            * score_scale
        )
        numbers = key_number(lax.broadcasted_iota(jnp.int32, (1, shard_piece.shape[0]), 1))
        exp_sums = jnp.sum(jnp.exp(scores), axis=1)
        picked = jnp.sum(jnp.where(targets[:, None] == numbers, scores, 0.0), axis=1)
        return (exp_sums, picked)

    return add_block


def same_number(gathered):
    return gathered


def body(
    pixels,
    depth_weight,
    mix_weight,
    spectral_real,
    spectral_imag,
    query_weight,
    key_weight,
    query_pixels,
    key_pixels,
    positives,
):
    slab_rows, groups, columns = pixels.shape
    half_cols = columns // 2
    channel = lax.axis_index("ch")
    group_count = lax.axis_size("ch")
    padded = extended(pixels, (("rows", 0),), DILATION)
    padded = jnp.pad(padded, ((0, 0), (0, 0), (DILATION, DILATION)))
    summed = pixels.astype(jnp.float32)
    for tap_row in range(3):
        for tap_col in range(3):
            shifted = padded[
                tap_row * DILATION : tap_row * DILATION + slab_rows,
                :,
                tap_col * DILATION : tap_col * DILATION + columns,
            ]
            summed = summed + depth_weight[:, 3 * tap_row + tap_col][
                None, :, None
            ] * shifted.astype(jnp.float32)
    conv_out = summed.astype(jnp.bfloat16)
    local_columns = lax.dynamic_slice_in_dim(mix_weight, channel * groups, groups, 1)
    mixture = jnp.einsum(
        "rcw,cd->rdw",
        lax.all_gather(conv_out, "ch", axis=1, tiled=True),
        local_columns,
        preferred_element_type=jnp.float32,
    )
    hidden = jax.nn.gelu(mixture).astype(jnp.bfloat16)
    spectrum_real, spectrum_imag = transform_last(
        hidden.astype(jnp.float32), None, -1.0, False, True
    )
    wire = jnp.stack([spectrum_real, spectrum_imag]).astype(jnp.bfloat16)
    columns_both = lax.all_to_all(wire, "rows", split_axis=3, concat_axis=1, tiled=True)
    column_real, column_imag = (columns_both[0], columns_both[1])
    full_real, full_imag = transform_first(
        column_real.astype(jnp.float32), column_imag.astype(jnp.float32), -1.0
    )
    kernel_real = spectral_real.astype(jnp.float32)
    kernel_imag = spectral_imag.astype(jnp.float32)
    product_real = full_real * kernel_real - full_imag * kernel_imag
    product_imag = full_real * kernel_imag + full_imag * kernel_real
    back_real, back_imag = transform_first(product_real, product_imag, 1.0)
    height = column_real.shape[0]
    back_real = (back_real * (1.0 / height)).astype(jnp.bfloat16)
    back_imag = (back_imag * (1.0 / height)).astype(jnp.bfloat16)
    rows_both = lax.all_to_all(
        jnp.stack([back_real, back_imag]), "rows", split_axis=1, concat_axis=3, tiled=True
    )
    row_real, row_imag = (rows_both[0], rows_both[1])
    doubling = jnp.where(lax.broadcasted_iota(jnp.int32, (1, 1, half_cols), 2) == 0, 1.0, 2.0)
    wide_real = jnp.pad(
        row_real.astype(jnp.float32) * doubling, ((0, 0), (0, 0), (0, columns - half_cols))
    )
    wide_imag = jnp.pad(
        row_imag.astype(jnp.float32) * doubling, ((0, 0), (0, 0), (0, columns - half_cols))
    )
    spatial = transform_last(wide_real, wide_imag, 1.0, True, False) * (1.0 / columns)
    encoded = (hidden.astype(jnp.float32) + spatial).astype(jnp.bfloat16)
    key_count = key_pixels.shape[0]
    query_count = query_pixels.shape[0]
    quarter = query_count // group_count
    slab = lax.axis_index("rows")
    weights_all = lax.all_gather(
        jnp.concatenate([key_weight, query_weight], axis=1), "ch", axis=0, tiled=True
    )
    sampled = jnp.concatenate([key_pixels, query_pixels])
    features = encoded[sampled // columns, :, sampled % columns]
    features = lax.all_gather(features, "ch", axis=1, tiled=True)
    key_dim = key_weight.shape[1]
    key_unit = unit_rows(
        jnp.dot(features[:key_count], weights_all[:, :key_dim], preferred_element_type=jnp.float32)
    ).astype(jnp.bfloat16)
    own_queries = lax.dynamic_slice_in_dim(features, key_count + channel * quarter, quarter, 0)
    query_unit = unit_rows(
        jnp.dot(own_queries, weights_all[:, key_dim:], preferred_element_type=jnp.float32)
    ).astype(jnp.bfloat16)
    targets = lax.dynamic_slice_in_dim(positives, channel * quarter, quarter, 0)
    coded = jnp.concatenate([targets // 128, targets % 128]).astype(jnp.bfloat16)
    coded = jnp.pad(coded, (0, key_dim - 2 * quarter))[None, :]
    packet = jnp.concatenate([query_unit, coded], axis=0)
    gathered = lax.all_gather(packet[None], "rows", axis=0, tiled=True)
    all_queries = gathered[:, :quarter, :].reshape(-1, key_dim)
    coded_all = gathered[:, quarter, :].astype(jnp.int32)
    all_targets = (coded_all[:, :quarter] * 128 + coded_all[:, quarter : 2 * quarter]).reshape(-1)
    scores = (
        jnp.einsum("qd,kd->qk", all_queries, key_unit, preferred_element_type=jnp.float32)
        * score_scale
    )
    numbers = slab * key_count + lax.broadcasted_iota(jnp.int32, (1, key_count), 1)
    exp_sums = jnp.sum(jnp.exp(scores), axis=1)
    picked = jnp.sum(jnp.where(all_targets[:, None] == numbers, scores, 0.0), axis=1)
    reduced = lax.psum_scatter(
        jnp.stack([exp_sums, picked], axis=1), "rows", scatter_dimension=0, tiled=True
    )
    losses = jnp.log(reduced[:, 0]) - reduced[:, 1]
    return (encoded, losses)


def solution(mesh):
    placed = (
        P("rows", "ch", None),
        P("ch", None),
        P(),
        P(None, "ch", "rows"),
        P(None, "ch", "rows"),
        P("ch", None),
        P("ch", None),
        P("rows"),
        P("rows"),
        P("rows"),
    )
    return jax.shard_map(
        body,
        mesh=mesh,
        in_specs=placed,
        out_specs=(P("rows", "ch", None), P(("rows", "ch"))),
        check_vma=False,
    )
```

profile of v0, /device:TPU:32, one launch (start us, length us, event | category | flops | bytes accessed | tf_op | source)
XLA Modules:
  0.0 866.5 jit_solution(4636469104525805419)
XLA Ops:
  17.9 56.4 %all-gather.4.cloned.1.call-done = bf16[4,96,2048]{2,1,0:T(8,128)(2,1)} async-done(((bf16[4,24,2048]{2,1,0:T(8,128)(2,1)}), bf16[4,96,2048]{2,1,0:T(8,128)(2,1)}) %all-gather.4.cloned.1.call-update) | async-done | bytes 1572880 | tf_op jit(solution)/shard_map/all_gather | solution.py:136
  83.1 2.7 fusion.83
  85.7 2.4 fusion.46
  92.4 3.8 fusion.45
  100.2 3.6 reshape.434
  103.8 11.1 %all-to-all-start = ((bf16[64,2,1536]{2,1,0:T(2,128)(2,1)}), bf16[64,2,1536]{2,1,0:T(2,128)(2,1)S(1)}, u32[]{:S(2)}, u32[]{:S(2)}) async-start(bf16[64,2,1536]{2,1,0:T(2,128)(2,1)} %reshape.434), calls=%async_computation | async-start | bytes 786432 | tf_op jit(solution)/shard_map/all_to_all | solution.py:145
  115.0 16.3 %all_gather.14 = bf16[96,256]{1,0:T(8,128)(2,1)S(1)} all-gather(bf16[24,256]{1,0:T(8,128)(2,1)S(1)} %pad_maximum_fusion.4), channel_id=1, replica_groups=mesh['rows'=64,'ch'=4] {'ch'}, dimensions={0}, use_global_device_ids=true | all-gather | bytes 61440 | tf_op jit(solution)/shard_map/all_gather | solution.py:175
  132.3 3.9 reshape.435
  136.2 5.5 copy.239
  141.7 2.8 fusion.321
  144.5 3.6 copy.177
  148.2 3.2 fusion.52
  153.3 4.1 copy.181
  161.7 2.4 fusion.12
  164.2 2.4 fusion.14
  166.6 3.8 subtract_bitcast_fusion
  170.4 4.0 add_bitcast_fusion
  174.4 3.8 copy.194
  180.3 3.8 copy.191
  187.6 2.6 reshape.392
  190.2 3.4 copy.195
  193.6 3.3 fusion.145
  196.9 3.3 fusion.151
  200.2 2.6 reshape.393
  202.8 3.8 copy.197
  206.7 3.8 convolution_subtract_fusion
  210.4 2.6 fusion
  213.1 2.4 fusion.4
  215.5 2.4 fusion.6
  217.9 2.7 fusion.42
  220.7 3.6 fusion.39
  224.3 3.9 copy.205
  229.7 2.7 copy.208
  234.0 3.1 copy.209
  237.1 3.6 reshape.436
  240.6 11.9 %all-to-all-start.1 = ((bf16[64,2,1536]{2,1,0:T(2,128)(2,1)}), bf16[64,2,1536]{2,1,0:T(2,128)(2,1)S(1)}, u32[]{:S(2)}, u32[]{:S(2)}) async-start(bf16[64,2,1536]{2,1,0:T(2,128)(2,1)} %reshape.436), calls=%async_computation.1 | async-start | bytes 786432 | tf_op jit(solution)/shard_map/all_to_all | solution.py:158
  252.9 17.5 %all-to-all-done.1 = bf16[64,2,1536]{2,1,0:T(2,128)(2,1)S(1)} async-done(((bf16[64,2,1536]{2,1,0:T(2,128)(2,1)}), bf16[64,2,1536]{2,1,0:T(2,128)(2,1)S(1)}, u32[]{:S(2)}, u32[]{:S(2)}) %all-to-all-start.1) | async-done | bytes 393248 | tf_op jit(solution)/shard_map/all_to_all | solution.py:158
  270.4 3.0 reshape.437
  273.4 2.6 copy.211
  279.3 3.3 reshape.398
  285.0 3.3 reshape.397
  290.9 2.7 fusion.120
  298.1 3.0 convolution_add_fusion.2
  304.4 2.8 multiply_bitcast_fusion
  314.0 4.9 gather_fusion
  319.0 12.0 %all_gather.13 = bf16[320,96]{0,1:T(8,128)(2,1)S(1)} all-gather(bf16[320,24]{0,1:T(8,128)(2,1)S(1)} %copy.218), channel_id=1, replica_groups=mesh['rows'=64,'ch'=4] {'ch'}, dimensions={1}, use_global_device_ids=true | all-gather | bytes 76800 | tf_op jit(solution)/shard_map/all_gather | solution.py:180
  331.7 110.5 %all-gather.1 = bf16[64,17,128]{2,1,0:T(8,128)(2,1)S(1)} all-gather(bf16[1,17,128]{2,1,0:T(8,128)(2,1)S(1)} %maximum_bitcast_fusion), channel_id=2, replica_groups=mesh['rows'=64,'ch'=4] {'rows'}, dimensions={0}, use_global_device_ids=true | all-gather | bytes 282880 | tf_op jit(solution)/shard_map/all_gather | solution.py:193
  443.9 414.0 %reduce-scatter.4.cloned.1.call-done = f32[16,2]{1,0:T(8,128)} async-done(((f32[1024,2]{1,0:T(8,128)}), f32[16,2]{1,0:T(8,128)}) %reduce-scatter.4.cloned.1.call-update) | async-done | bytes 144
  (108 shorter events, 70.7 us)
Async XLA Ops:
  7.2 67.2 %copy-start = (bf16[96,96]{1,0:T(8,128)(2,1)S(1)}, bf16[96,96]{1,0:T(8,128)(2,1)}, u32[]{:S(2)}) copy-start(bf16[96,96]{1,0:T(8,128)(2,1)} %param.12) | copy-start | bytes 55300
  7.2 8.8 %copy-start.5 = (bf16[4,24,2048]{2,1,0:T(8,128)(2,1)S(1)}, bf16[4,24,2048]{2,1,0:T(8,128)(2,1)}, u32[]{:S(2)}) copy-start(bf16[4,24,2048]{2,1,0:T(8,128)(2,1)} %param.10) | copy-start | bytes 1179652
  7.2 67.1 %all-gather.4.cloned.1.call-start = ((), (), s32[]{:S(2)}) async-start(), calls=%async_computation.3 | async-start | bytes 1966080 | tf_op jit(solution)/shard_map/all_gather | solution.py:136
  8.3 4.0 collective-permute-start
  10.1 4.6 collective-permute-start.1
  76.3 0.8 copy-start.7
  77.9 0.9 copy-start.4
  100.2 14.7 %copy-start.12 = (s32[256]{0:T(256)S(1)}, s32[256]{0:T(256)}, u32[]{:S(2)}) copy-start(s32[256]{0:T(256)} %param.18) | copy-start | bytes 3076
  100.2 14.7 %copy-start.13 = (s32[64]{0:T(128)S(1)}, s32[64]{0:T(128)}, u32[]{:S(2)}) copy-start(s32[64]{0:T(128)} %param.17) | copy-start | bytes 772
  100.2 14.8 %copy-start.10 = (bf16[24,128]{1,0:T(8,128)(2,1)S(1)}, bf16[24,128]{1,0:T(8,128)(2,1)}, u32[]{:S(2)}) copy-start(bf16[24,128]{1,0:T(8,128)(2,1)} %param.15) | copy-start | bytes 18436
  100.2 14.7 %copy-start.11 = (bf16[24,128]{1,0:T(8,128)(2,1)S(1)}, bf16[24,128]{1,0:T(8,128)(2,1)}, u32[]{:S(2)}) copy-start(bf16[24,128]{1,0:T(8,128)(2,1)} %param.16) | copy-start | bytes 18436
  103.8 28.5 %all-to-all-start = ((bf16[64,2,1536]{2,1,0:T(2,128)(2,1)}), bf16[64,2,1536]{2,1,0:T(2,128)(2,1)S(1)}, u32[]{:S(2)}, u32[]{:S(2)}) async-start(bf16[64,2,1536]{2,1,0:T(2,128)(2,1)} %reshape.434), calls=%async_computation | async-start | bytes 786432 | tf_op jit(solution)/shard_map/all_to_all | solution.py:145
  157.4 2.0 copy-start.3
  184.1 2.1 copy-start.9
  206.6 3.8 copy-start.2
  237.0 15.5 %copy-start.14 = (s32[64]{0:T(128)S(1)}, s32[64]{0:T(128)}, u32[]{:S(2)}) copy-start(s32[64]{0:T(128)} %param.19) | copy-start | bytes 772
  240.6 29.8 %all-to-all-start.1 = ((bf16[64,2,1536]{2,1,0:T(2,128)(2,1)}), bf16[64,2,1536]{2,1,0:T(2,128)(2,1)S(1)}, u32[]{:S(2)}, u32[]{:S(2)}) async-start(bf16[64,2,1536]{2,1,0:T(2,128)(2,1)} %reshape.436), calls=%async_computation.1 | async-start | bytes 786432 | tf_op jit(solution)/shard_map/all_to_all | solution.py:158
  252.5 605.5 %reduce-scatter.4.cloned.1.call-start = ((), (), s32[]{:S(2)}) async-start(), calls=%async_computation.4 | async-start | bytes 532480
  293.6 1.5 copy-start.8
  313.0 129.2 %copy-start.6 = (bf16[4,24,2048]{2,1,0:T(8,128)(2,1)}, bf16[4,24,2048]{2,1,0:T(8,128)(2,1)S(1)}, u32[]{:S(2)}) copy-start(bf16[4,24,2048]{2,1,0:T(8,128)(2,1)S(1)} %add_convert_fusion.1) | copy-start | bytes 1179652
  331.6 527.9 %copy-start.1 = (bf16[96,96]{1,0:T(8,128)(2,1)S(1)}, bf16[96,96]{1,0:T(8,128)(2,1)}, u32[]{:S(2)}) copy-start(bf16[96,96]{1,0:T(8,128)(2,1)} %param.12) | copy-start | bytes 55300
Sparse Core Ops, SparseCore 0:
  17.9 56.3 all-gather.3
  444.1 413.8 reduce-scatter.3
where the time goes:
time: 876 us; the launch traced here: 867 us
  waiting for transfers between devices  491 us (56%)
  blocking collectives  139 us (16%)
  local copies, waits for them, and re-layouts  109 us (12%)
  matrix products  75.7 us (9%)
  starting transfers between devices  26.1 us (3%)
  between operations  14.9 us (2%)
  other arithmetic  10.4 us (1%)
    unnamed x3, waiting for transfers between devices  414 us
    all_gather x1, blocking collectives, body(): gathered = lax.all_gather(packet[None], 'rows', axis=0, tiled=True)  110 us
    all_gather x1, waiting for transfers between devices, body(): lax.all_gather(conv_out, 'ch', axis=1, tiled=True)  56.4 us
    dot_general x14, matrix products, over_second(): return jnp.einsum('...kb,bm->...km', values, matrix, precision=exact)  38.5 us
    dot_general x14, matrix products, over_first(): return jnp.einsum('ka,...ab->...kb', matrix, values, precision=exact)  34.2 us
    all_to_all x1, waiting for transfers between devices, body(): lax.all_to_all(jnp.stack([back_real, back_imag]), 'rows', split_axis=1, c...  17.5 us
  transfers between devices with their start and end apart: 6, of which 5 were waited for; matrix products, arithmetic and copies ran while one was open for 0% of the time, Pallas kernels for 0%

commit v1 on v0

--- a/solution.py
+++ b/solution.py
@@ -190,7 +190,9 @@
     coded = jnp.concatenate([targets // 128, targets % 128]).astype(jnp.bfloat16)
     coded = jnp.pad(coded, (0, key_dim - 2 * quarter))[None, :]
     packet = jnp.concatenate([query_unit, coded], axis=0)
-    gathered = lax.all_gather(packet[None], "rows", axis=0, tiled=True)
+    gathered = jnp.concatenate(
+        lax.all_to_all(jnp.stack(lax.psum(1, "rows") * [packet[None]], axis=0), "rows", 0, 0), 0
+    )
     all_queries = gathered[:, :quarter, :].reshape(-1, key_dim)
     coded_all = gathered[:, quarter, :].astype(jnp.int32)
     all_targets = (coded_all[:, :quarter] * 128 + coded_all[:, quarter : 2 * quarter]).reshape(-1)

time: 876 us -> 787 us (0.90)
  blocking collectives: 139 us -> 28.6 us
  waiting for transfers between devices: 491 us -> 506 us
    all_gather x1 -> x0, blocking collectives: 110 us -> none  [body(): gathered = lax.all_gather(packet[None], 'rows', axis=0, tiled=True)]
    all_to_all x0 -> x1, waiting for transfers between devices: none -> 17.8 us  [body(): lax.all_to_all(jnp.stack(lax.psum(1, 'rows') * [packet[None]], axis=0), '...]
    all_to_all x1, waiting for transfers between devices: 0.89 us -> 17.4 us  [body(): lax.all_to_all(wire, 'rows', split_axis=3, concat_axis=1, tiled=True)]
    all_to_all x1, waiting for transfers between devices: 17.5 us -> 1.53 us  [body(): lax.all_to_all(jnp.stack([back_real, back_imag]), 'rows', split_axis=1, c...]
    all_to_all x0 -> x1, starting transfers between devices: none -> 12.8 us  [body(): lax.all_to_all(jnp.stack(lax.psum(1, 'rows') * [packet[None]], axis=0), '...]
  transfers between devices with their start and end apart: 6 -> 7, of which waited for: 5 -> 6; matrix products, arithmetic and copies ran while one was open for 0% -> 0% of each run, Pallas kernels for 0% -> 0%
where the time goes in v1:
time: 787 us; the launch traced here: 778 us
  waiting for transfers between devices  506 us (64%)
  local copies, waits for them, and re-layouts  110 us (14%)
  matrix products  75.8 us (10%)
  starting transfers between devices  31.8 us (4%)
  blocking collectives  28.6 us (4%)
  between operations  14.9 us (2%)
  other arithmetic  10.4 us (1%)
    unnamed x3, waiting for transfers between devices  410 us
    all_gather x1, waiting for transfers between devices, body(): lax.all_gather(conv_out, 'ch', axis=1, tiled=True)  56.4 us
    dot_general x14, matrix products, over_second(): return jnp.einsum('...kb,bm->...km', values, matrix, precision=exact)  38.6 us
    dot_general x14, matrix products, over_first(): return jnp.einsum('ka,...ab->...kb', matrix, values, precision=exact)  34.2 us
    all_to_all x1, waiting for transfers between devices, body(): lax.all_to_all(jnp.stack(lax.psum(1, 'rows') * [packet[None]], axis=0), '...  17.8 us
    all_to_all x1, waiting for transfers between devices, body(): lax.all_to_all(wire, 'rows', split_axis=3, concat_axis=1, tiled=True)  17.4 us
    unnamed x37, local copies, waits for them, and re-layouts  17 us
    all_gather x1, blocking collectives, body(): lax.all_gather(jnp.concatenate([key_weight, query_weight], axis=1), 'ch',...  16.9 us
  transfers between devices with their start and end apart: 7, of which 6 were waited for; matrix products, arithmetic and copies ran while one was open for 0% of the time, Pallas kernels for 0%

profile of v1, /device:TPU:32, one launch (start us, length us, event | category | flops | bytes accessed | tf_op | source)
XLA Modules:
  0.0 777.6 jit_solution(9291709852071003650)
XLA Ops:
  17.9 56.4 %all-gather.2.cloned.1.call-done = bf16[4,96,2048]{2,1,0:T(8,128)(2,1)} async-done(((bf16[4,24,2048]{2,1,0:T(8,128)(2,1)}), bf16[4,96,2048]{2,1,0:T(8,128)(2,1)}) %all-gather.2.cloned.1.call-update) | async-done | bytes 1572880 | tf_op jit(solution)/shard_map/all_gather | solution.py:136
  83.1 2.7 fusion.83
  85.8 2.4 fusion.46
  92.5 3.8 fusion.45
  100.3 3.6 reshape.436
  103.8 11.0 %all-to-all-start = ((bf16[64,2,1536]{2,1,0:T(2,128)(2,1)}), bf16[64,2,1536]{2,1,0:T(2,128)(2,1)S(1)}, u32[]{:S(2)}, u32[]{:S(2)}) async-start(bf16[64,2,1536]{2,1,0:T(2,128)(2,1)} %reshape.436), calls=%async_computation | async-start | bytes 786432 | tf_op jit(solution)/shard_map/all_to_all | solution.py:145
  115.1 17.4 %all-to-all-done = bf16[64,2,1536]{2,1,0:T(2,128)(2,1)S(1)} async-done(((bf16[64,2,1536]{2,1,0:T(2,128)(2,1)}), bf16[64,2,1536]{2,1,0:T(2,128)(2,1)S(1)}, u32[]{:S(2)}, u32[]{:S(2)}) %all-to-all-start) | async-done | bytes 393248 | tf_op jit(solution)/shard_map/all_to_all | solution.py:145
  132.4 3.9 reshape.437
  136.4 5.5 copy.281
  141.8 2.8 fusion.321
  144.6 3.6 copy.219
  148.3 3.2 fusion.52
  153.5 4.1 copy.223
  161.9 2.4 fusion.12
  166.8 3.8 subtract_bitcast_fusion
  170.5 4.0 add_bitcast_fusion
  174.5 3.8 copy.236
  180.5 3.8 copy.233
  187.7 2.6 reshape.397
  190.4 3.4 copy.237
  193.8 3.3 fusion.145
  197.1 3.3 fusion.151
  200.4 2.6 reshape.398
  203.0 3.8 copy.239
  206.9 3.8 convolution_subtract_fusion
  210.6 2.6 fusion
  213.3 2.4 fusion.4
  215.7 2.4 fusion.6
  218.2 2.7 fusion.42
  220.9 3.6 fusion.39
  224.5 3.9 copy.247
  229.9 2.7 copy.250
  234.1 3.1 copy.251
  237.3 3.6 reshape.438
  240.9 4.8 all-to-all-start.1
  245.7 16.9 %all_gather.11 = bf16[96,256]{1,0:T(8,128)(2,1)S(1)} all-gather(bf16[24,256]{1,0:T(8,128)(2,1)S(1)} %pad_maximum_fusion.4), channel_id=1, replica_groups=mesh['rows'=64,'ch'=4] {'ch'}, dimensions={0}, use_global_device_ids=true | all-gather | bytes 61440 | tf_op jit(solution)/shard_map/all_gather | solution.py:175
  264.4 3.0 reshape.439
  267.4 2.6 copy.253
  273.3 3.3 reshape.404
  279.0 3.3 reshape.403
  284.9 2.7 fusion.120
  292.1 3.0 convolution_add_fusion.2
  298.4 2.8 multiply_bitcast_fusion
  308.1 4.9 gather_fusion
  313.0 11.7 %all_gather.10 = bf16[320,96]{0,1:T(8,128)(2,1)S(1)} all-gather(bf16[320,24]{0,1:T(8,128)(2,1)S(1)} %copy.260), channel_id=1, replica_groups=mesh['rows'=64,'ch'=4] {'ch'}, dimensions={1}, use_global_device_ids=true | all-gather | bytes 76800 | tf_op jit(solution)/shard_map/all_gather | solution.py:180
  326.0 12.8 %all-to-all-start.2 = ((bf16[64,1,17,128]{3,2,1,0:T(8,128)(2,1)}), bf16[64,1,17,128]{3,2,1,0:T(8,128)(2,1)S(1)}, u32[]{:S(2)}, u32[]{:S(2)}) async-start(bf16[64,1,17,128]{3,2,1,0:T(8,128)(2,1)} %stack.29), calls=%async_computation.2 | async-start | bytes 786432 | tf_op jit(solution)/shard_map/all_to_all | solution.py:194
  339.1 17.8 %all-to-all-done.2 = bf16[64,1,17,128]{3,2,1,0:T(8,128)(2,1)S(1)} async-done(((bf16[64,1,17,128]{3,2,1,0:T(8,128)(2,1)}), bf16[64,1,17,128]{3,2,1,0:T(8,128)(2,1)S(1)}, u32[]{:S(2)}, u32[]{:S(2)}) %all-to-all-start.2) | async-done | bytes 278560 | tf_op jit(solution)/shard_map/all_to_all | solution.py:194
  358.7 410.4 %reduce-scatter.4.cloned.1.call-done = f32[16,2]{1,0:T(8,128)} async-done(((f32[1024,2]{1,0:T(8,128)}), f32[16,2]{1,0:T(8,128)}) %reduce-scatter.4.cloned.1.call-update) | async-done | bytes 144
  (110 shorter events, 74.6 us)
Async XLA Ops:
  7.2 67.2 %copy-start = (bf16[96,96]{1,0:T(8,128)(2,1)S(1)}, bf16[96,96]{1,0:T(8,128)(2,1)}, u32[]{:S(2)}) copy-start(bf16[96,96]{1,0:T(8,128)(2,1)} %param.12) | copy-start | bytes 55300
  7.2 8.8 %copy-start.5 = (bf16[4,24,2048]{2,1,0:T(8,128)(2,1)S(1)}, bf16[4,24,2048]{2,1,0:T(8,128)(2,1)}, u32[]{:S(2)}) copy-start(bf16[4,24,2048]{2,1,0:T(8,128)(2,1)} %param.10) | copy-start | bytes 1179652
  7.2 67.1 %all-gather.2.cloned.1.call-start = ((), (), s32[]{:S(2)}) async-start(), calls=%async_computation.4 | async-start | bytes 1966080 | tf_op jit(solution)/shard_map/all_gather | solution.py:136
  8.3 4.0 collective-permute-start
  10.1 4.6 collective-permute-start.1
  76.3 0.8 copy-start.7
  77.9 0.9 copy-start.4
  100.2 14.6 %copy-start.12 = (s32[256]{0:T(256)S(1)}, s32[256]{0:T(256)}, u32[]{:S(2)}) copy-start(s32[256]{0:T(256)} %param.18) | copy-start | bytes 3076
  100.2 14.6 %copy-start.13 = (s32[64]{0:T(128)S(1)}, s32[64]{0:T(128)}, u32[]{:S(2)}) copy-start(s32[64]{0:T(128)} %param.17) | copy-start | bytes 772
  103.8 28.6 %all-to-all-start = ((bf16[64,2,1536]{2,1,0:T(2,128)(2,1)}), bf16[64,2,1536]{2,1,0:T(2,128)(2,1)S(1)}, u32[]{:S(2)}, u32[]{:S(2)}) async-start(bf16[64,2,1536]{2,1,0:T(2,128)(2,1)} %reshape.436), calls=%async_computation | async-start | bytes 786432 | tf_op jit(solution)/shard_map/all_to_all | solution.py:145
  157.5 2.0 copy-start.3
  184.3 2.1 copy-start.9
  206.8 3.8 copy-start.2
  237.2 8.5 %copy-start.10 = (bf16[24,128]{1,0:T(8,128)(2,1)S(1)}, bf16[24,128]{1,0:T(8,128)(2,1)}, u32[]{:S(2)}) copy-start(bf16[24,128]{1,0:T(8,128)(2,1)} %param.15) | copy-start | bytes 18436
  237.2 8.5 %copy-start.11 = (bf16[24,128]{1,0:T(8,128)(2,1)S(1)}, bf16[24,128]{1,0:T(8,128)(2,1)}, u32[]{:S(2)}) copy-start(bf16[24,128]{1,0:T(8,128)(2,1)} %param.16) | copy-start | bytes 18436
  237.3 25.4 %copy-start.14 = (s32[64]{0:T(128)S(1)}, s32[64]{0:T(128)}, u32[]{:S(2)}) copy-start(s32[64]{0:T(128)} %param.19) | copy-start | bytes 772
  240.9 23.6 %all-to-all-start.1 = ((bf16[64,2,1536]{2,1,0:T(2,128)(2,1)}), bf16[64,2,1536]{2,1,0:T(2,128)(2,1)S(1)}, u32[]{:S(2)}, u32[]{:S(2)}) async-start(bf16[64,2,1536]{2,1,0:T(2,128)(2,1)} %reshape.438), calls=%async_computation.1 | async-start | bytes 786432 | tf_op jit(solution)/shard_map/all_to_all | solution.py:158
  287.6 1.5 copy-start.8
  307.0 19.0 %copy-start.6 = (bf16[4,24,2048]{2,1,0:T(8,128)(2,1)}, bf16[4,24,2048]{2,1,0:T(8,128)(2,1)S(1)}, u32[]{:S(2)}) copy-start(bf16[4,24,2048]{2,1,0:T(8,128)(2,1)S(1)} %add_convert_fusion.1) | copy-start | bytes 1179652
  326.0 30.9 %all-to-all-start.2 = ((bf16[64,1,17,128]{3,2,1,0:T(8,128)(2,1)}), bf16[64,1,17,128]{3,2,1,0:T(8,128)(2,1)S(1)}, u32[]{:S(2)}, u32[]{:S(2)}) async-start(bf16[64,1,17,128]{3,2,1,0:T(8,128)(2,1)} %stack.29), calls=%async_computation.2 | async-start | bytes 786432 | tf_op jit(solution)/shard_map/all_to_all | solution.py:194
  338.8 431.8 %copy-start.1 = (bf16[96,96]{1,0:T(8,128)(2,1)S(1)}, bf16[96,96]{1,0:T(8,128)(2,1)}, u32[]{:S(2)}) copy-start(bf16[96,96]{1,0:T(8,128)(2,1)} %param.12) | copy-start | bytes 55300
  338.8 430.3 %reduce-scatter.4.cloned.1.call-start = ((), (), s32[]{:S(2)}) async-start(), calls=%async_computation.5 | async-start | bytes 532480
Sparse Core Ops, SparseCore 0:
  17.9 56.3 all-gather.1
  358.8 410.2 reduce-scatter.3
